TPU v7x, 32 devices: a whole 2x2x4 slice. The times are simulated.
32 devices in a mesh: shard: 4 (over x, core), ctx: 8 (over z, y).
Axes of the slice: x: 2, y: 2, z: 4, core: 2. Of those that a mesh axis runs over, the one named last changes fastest.
Arguments:
- tokens: bfloat16 [4, 1024, 768], P('shard', 'ctx'), may hold values from -6 to 6
- segments: int32 [4, 1024], P('shard', 'ctx'), may hold values from 0 to 11, never falling along the last dimension, each value on 1 to 640 neighbouring positions
- joint_weight: float32 [768, 2304], P(('shard', 'ctx')), may hold values from -0.21875 to 0.21875
- query_bias: float32 [768], P(('shard', 'ctx')), may hold values from -3 to 3
- value_bias: float32 [768], P(('shard', 'ctx')), may hold values from -1.75 to 1.75
- out_weight: float32 [768, 768], P(('shard', 'ctx')), may hold values from -1.75 to 1.75
- out_bias: float32 [768], P(('shard', 'ctx')), may hold values from -1.75 to 1.75
- mid_gain: float32 [768], P(('shard', 'ctx')), may hold values from 0.1 to 1.9
- mid_shift: float32 [768], P(('shard', 'ctx')), may hold values from -3 to 3
- up_weight: float32 [768, 3072], P(('shard', 'ctx')), may hold values from -0.21875 to 0.21875
- up_bias: float32 [3072], P(('shard', 'ctx')), may hold values from -3 to 3
- down_weight: float32 [3072, 768], P(('shard', 'ctx')), may hold values from -0.109375 to 0.109375
- down_bias: float32 [768], P(('shard', 'ctx')), may hold values from -3 to 3
- final_gain: float32 [768], P(('shard', 'ctx')), may hold values from 0.1 to 1.9
- final_shift: float32 [768], P(('shard', 'ctx')), may hold values from -3 to 3
- cotangent: bfloat16 [4, 1024, 768], P('shard', 'ctx'), may hold values from -6 to 6
Outputs:
- layer_output: bfloat16 [4, 1024, 768], P('shard', 'ctx')
- input_grad: bfloat16 [4, 1024, 768], P('shard', 'ctx')
- grad_joint_weight: float32 [768, 2304], P(('shard', 'ctx'))
- grad_query_bias: float32 [768], P(('shard', 'ctx'))
- grad_value_bias: float32 [768], P(('shard', 'ctx'))
- grad_out_weight: float32 [768, 768], P(('shard', 'ctx'))
- grad_out_bias: float32 [768], P(('shard', 'ctx'))
- grad_mid_gain: float32 [768], P(('shard', 'ctx'))
- grad_mid_shift: float32 [768], P(('shard', 'ctx'))
- grad_up_weight: float32 [768, 3072], P(('shard', 'ctx'))
- grad_up_bias: float32 [3072], P(('shard', 'ctx'))
- grad_down_weight: float32 [3072, 768], P(('shard', 'ctx'))
- grad_down_bias: float32 [768], P(('shard', 'ctx'))
- grad_final_gain: float32 [768], P(('shard', 'ctx'))
- grad_final_shift: float32 [768], P(('shard', 'ctx'))
Inputs may be any that keep to these rules, and one draw needn't show every extreme that they name: `segments`: along each sequence the ids never fall; there are 12 documents of 1 to 640 positions, and one of exactly 640 in every sequence.
All inputs are finite; a program needn't handle non-finite values.
Results may differ from a plain program's by a relative error of at most 0.024.
Values may be sent and summed in bfloat16 or wider, within the bound.
No kernel may reach another device: no remote copies, remote signals or barrier semaphores. Data moves between devices by JAX's collectives and lax.ppermute only.
A program may use at most 192 MiB of HBM per device.

v0:
```python
import math

import jax
import jax.numpy as jnp
from jax import lax
from jax.sharding import PartitionSpec as P

HEADS = 12


MASKED = -1e30
EPSILON = 1e-05


def halve(master):
    return master.astype(jnp.bfloat16)


def widen(vector):
    return vector.astype(jnp.float32)


def smooth_gate(value):
    return jax.nn.gelu(value, approximate=False)


def normalize_fwd(hidden, gain, shift):
    center = hidden - jnp.mean(hidden, axis=-1, keepdims=True)
    inverse_dev = lax.rsqrt(jnp.mean(center * center, axis=-1, keepdims=True) + EPSILON)
    normed = center * inverse_dev
    return (normed * gain + shift, normed, inverse_dev)


def normalize_back(upstream, normed, inverse_dev, gain):
    scaled = upstream * gain
    inner = (
        scaled
        - jnp.mean(scaled, axis=-1, keepdims=True)
        - normed * jnp.mean(scaled * normed, axis=-1, keepdims=True)
    )
    return (inner * inverse_dev, jnp.sum(upstream * normed, axis=0), jnp.sum(upstream, axis=0))


def masked_logits(query_heads, query_docs, key_block, key_docs):
    groups, key_count, model_width = key_block.shape
    head_count = query_heads.shape[2]
    head_dim = model_width // head_count
    key_heads = key_block.reshape(groups, key_count, head_count, head_dim)
    logits = jnp.einsum(
        "sqhe,skhe->shqk", query_heads, key_heads, preferred_element_type=jnp.float32
    ) * head_dim ** (-0.5)
    same_doc = query_docs[:, None, :, None] == key_docs[:, None, None, :]
    return jnp.where(same_doc, logits, MASKED)


def absorb(running, key_block, value_block, key_docs, query_heads, query_docs):
    row_max, row_sum, weighted = running
    groups, key_count, model_width = value_block.shape
    head_count = query_heads.shape[2]
    head_dim = model_width // head_count
    tok_count = weighted.shape[1]
    logits = masked_logits(query_heads, query_docs, key_block, key_docs)
    new_max = jnp.maximum(row_max, jnp.max(logits, axis=-1))
    weights = jnp.exp(logits - new_max[..., None])
    factor = jnp.exp(row_max - new_max)
    new_sum = row_sum * factor + jnp.sum(weights, axis=-1)
    value_heads = value_block.reshape(groups, key_count, head_count, head_dim)
    partial_value = jnp.einsum(
        "shqk,skhe->sqhe",
        weights.astype(jnp.bfloat16),
        value_heads,
        preferred_element_type=jnp.float32,
    )
    scaled = (
        weighted.reshape(groups, tok_count, head_count, head_dim)
        * jnp.transpose(factor, (0, 2, 1))[..., None]
    )
    return (new_max, new_sum, (scaled + partial_value).reshape(groups, tok_count, model_width))


def absorb_all(running, piece_tuple, query_heads, query_docs):
    key_part, value_part, docs_part = piece_tuple
    key_count = key_part.shape[1]
    block_len = key_count if key_count <= 1024 else math.gcd(key_count, 512)
    if block_len == key_count:
        return absorb(running, key_part, value_part, docs_part, query_heads, query_docs)

    def loop_step(block_index, current):
        begin = block_index * block_len
        return absorb(
            current,
            lax.dynamic_slice_in_dim(key_part, begin, block_len, 1),
            lax.dynamic_slice_in_dim(value_part, begin, block_len, 1),
            lax.dynamic_slice_in_dim(docs_part, begin, block_len, 1),
            query_heads,
            query_docs,
        )

    return lax.fori_loop(0, key_count // block_len, loop_step, running)


def local(
    tokens,
    segments,
    joint_weight,
    query_bias,
    value_bias,
    out_weight,
    out_bias,
    mid_gain,
    mid_shift,
    up_weight,
    up_bias,
    down_weight,
    down_bias,
    final_gain,
    final_shift,
    cotangent,
):
    seq_count, tok_count, model_width = tokens.shape
    head_count = HEADS
    head_dim = model_width // head_count
    key_scale = head_dim ** (-0.5)
    row_count = seq_count * tok_count
    (
        joint_low,
        query_bias_low,
        value_bias_low,
        out_low,
        out_bias_low,
        mid_gain_low,
        mid_shift_low,
        up_low,
        up_bias_low,
        down_low,
        down_bias_low,
        final_gain_low,
        final_shift_low,
    ) = (
        lax.all_gather(halve(joint_weight), ("shard", "ctx"), axis=0, tiled=True),
        lax.all_gather(halve(query_bias), ("shard", "ctx"), axis=0, tiled=True),
        lax.all_gather(halve(value_bias), ("shard", "ctx"), axis=0, tiled=True),
        lax.all_gather(halve(out_weight), ("shard", "ctx"), axis=0, tiled=True),
        lax.all_gather(halve(out_bias), ("shard", "ctx"), axis=0, tiled=True),
        lax.all_gather(halve(mid_gain), ("shard", "ctx"), axis=0, tiled=True),
        lax.all_gather(halve(mid_shift), ("shard", "ctx"), axis=0, tiled=True),
        lax.all_gather(halve(up_weight), ("shard", "ctx"), axis=0, tiled=True),
        lax.all_gather(halve(up_bias), ("shard", "ctx"), axis=0, tiled=True),
        lax.all_gather(halve(down_weight), ("shard", "ctx"), axis=0, tiled=True),
        lax.all_gather(halve(down_bias), ("shard", "ctx"), axis=0, tiled=True),
        lax.all_gather(halve(final_gain), ("shard", "ctx"), axis=0, tiled=True),
        lax.all_gather(halve(final_shift), ("shard", "ctx"), axis=0, tiled=True),
    )
    flat_tokens = tokens.reshape(row_count, model_width)
    joint_shift = jnp.concatenate(
        [widen(query_bias_low), jnp.zeros((model_width,), jnp.float32), widen(value_bias_low)]
    )
    projected = (
        jnp.dot(flat_tokens, joint_low, preferred_element_type=jnp.float32) + joint_shift
    ).astype(jnp.bfloat16)
    projected = projected.reshape(seq_count, tok_count, 3 * model_width)
    query_low = projected[:, :, :model_width]
    key_low = projected[:, :, model_width : 2 * model_width]
    value_low = projected[:, :, 2 * model_width :]
    query_heads = query_low.reshape(seq_count, tok_count, head_count, head_dim)
    starting = (
        jnp.full((seq_count, head_count, tok_count), MASKED, jnp.float32),
        jnp.zeros((seq_count, head_count, tok_count), jnp.float32),
        jnp.zeros((seq_count, tok_count, model_width), jnp.float32),
    )
    running = absorb_all(
        starting,
        (
            lax.all_gather(key_low, "ctx", axis=1, tiled=True),
            lax.all_gather(value_low, "ctx", axis=1, tiled=True),
            lax.all_gather(segments, "ctx", axis=1, tiled=True),
        ),
        query_heads,
        segments,
    )
    row_max, row_sum, weighted = running
    inverse_sum = jnp.transpose(1.0 / row_sum, (0, 2, 1))[..., None]
    attended = (weighted.reshape(seq_count, tok_count, head_count, head_dim) * inverse_sum).reshape(
        seq_count, tok_count, model_width
    )
    log_norm = row_max + jnp.log(row_sum)
    attended_low = attended.astype(jnp.bfloat16).reshape(row_count, model_width)
    attn_branch = jnp.dot(attended_low, out_low, preferred_element_type=jnp.float32) + widen(
        out_bias_low
    )
    mid_value, mid_normed, mid_inverse = normalize_fwd(
        widen(flat_tokens) + attn_branch, widen(mid_gain_low), widen(mid_shift_low)
    )
    mid_low = mid_value.astype(jnp.bfloat16)
    up_value = jnp.dot(mid_low, up_low, preferred_element_type=jnp.float32) + widen(up_bias_low)
    activated, gate_back = jax.vjp(smooth_gate, up_value)
    activated_low = activated.astype(jnp.bfloat16)
    ffn_branch = jnp.dot(activated_low, down_low, preferred_element_type=jnp.float32) + widen(
        down_bias_low
    )
    final_value, final_normed, final_inverse = normalize_fwd(
        mid_value + ffn_branch, widen(final_gain_low), widen(final_shift_low)
    )
    layer_output = final_value.astype(jnp.bfloat16).reshape(seq_count, tok_count, model_width)
    back_joint, back_out, back_mid_gain, back_up, back_down, back_final_gain = (
        lax.all_gather(halve(joint_weight), ("shard", "ctx"), axis=0, tiled=True),
        lax.all_gather(halve(out_weight), ("shard", "ctx"), axis=0, tiled=True),
        lax.all_gather(halve(mid_gain), ("shard", "ctx"), axis=0, tiled=True),
        lax.all_gather(halve(up_weight), ("shard", "ctx"), axis=0, tiled=True),
        lax.all_gather(halve(down_weight), ("shard", "ctx"), axis=0, tiled=True),
        lax.all_gather(halve(final_gain), ("shard", "ctx"), axis=0, tiled=True),
    )
    grad_output = widen(cotangent.reshape(row_count, model_width))
    grad_final, grad_final_gain, grad_final_shift = normalize_back(
        grad_output, final_normed, final_inverse, widen(back_final_gain)
    )
    grad_ffn = grad_final.astype(jnp.bfloat16)
    grad_down_weight = jnp.einsum(
        "rf,rd->fd", activated_low, grad_ffn, preferred_element_type=jnp.float32
    )
    grad_down_bias = jnp.sum(widen(grad_ffn), axis=0)
    grad_act = jnp.einsum("rd,fd->rf", grad_ffn, back_down, preferred_element_type=jnp.float32)
    grad_up = gate_back(grad_act)[0].astype(jnp.bfloat16)
    grad_up_weight = jnp.einsum("rd,rf->df", mid_low, grad_up, preferred_element_type=jnp.float32)
    grad_up_bias = jnp.sum(widen(grad_up), axis=0)
    grad_mid = grad_final + jnp.einsum(
        "rf,df->rd", grad_up, back_up, preferred_element_type=jnp.float32
    )
    grad_hidden, grad_mid_gain, grad_mid_shift = normalize_back(
        grad_mid, mid_normed, mid_inverse, widen(back_mid_gain)
    )
    grad_attn = grad_hidden.astype(jnp.bfloat16)
    grad_out_weight = jnp.einsum(
        "rd,re->de", attended_low, grad_attn, preferred_element_type=jnp.float32
    )
    grad_out_bias = jnp.sum(widen(grad_attn), axis=0)
    grad_mixed = jnp.einsum(
        "re,de->rd", grad_attn, back_out, preferred_element_type=jnp.float32
    ).astype(jnp.bfloat16)
    grad_mixed = grad_mixed.reshape(seq_count, tok_count, model_width)
    grad_heads = grad_mixed.reshape(seq_count, tok_count, head_count, head_dim)
    delta_rows = jnp.sum(
        (widen(grad_mixed) * attended).reshape(seq_count, tok_count, head_count, head_dim), axis=-1
    )
    delta_rows = jnp.transpose(delta_rows, (0, 2, 1))
    own_delta = delta_rows
    all_keys = lax.all_gather(key_low, "ctx", axis=1, tiled=True)
    all_values = lax.all_gather(value_low, "ctx", axis=1, tiled=True)
    all_docs = lax.all_gather(segments, "ctx", axis=1, tiled=True)
    total_keys = all_keys.shape[1]
    block_len = math.gcd(total_keys, 512)

    def block_terms_of(begin):
        key_block = lax.dynamic_slice_in_dim(all_keys, begin, block_len, 1)
        value_block = lax.dynamic_slice_in_dim(all_values, begin, block_len, 1)
        docs_block = lax.dynamic_slice_in_dim(all_docs, begin, block_len, 1)
        logits = masked_logits(query_heads, segments, key_block, docs_block)
        probs = jnp.exp(logits - log_norm[..., None])
        key_heads = key_block.reshape(1, block_len, head_count, head_dim)
        value_heads = value_block.reshape(1, block_len, head_count, head_dim)
        grad_probs = jnp.einsum(
            "sqhe,skhe->shqk", grad_heads, value_heads, preferred_element_type=jnp.float32
        )
        score_grad = (probs * (grad_probs - own_delta[..., None])).astype(jnp.bfloat16)
        return (probs, score_grad, key_heads)

    def key_step(block_index, tallies):
        query_tally, pair_tally = tallies
        begin = block_index * block_len
        probs, score_grad, key_heads = block_terms_of(begin)
        query_tally = query_tally + jnp.einsum(
            "shqk,skhe->sqhe", score_grad, key_heads, preferred_element_type=jnp.float32
        )
        key_term = jnp.einsum(
            "shqk,sqhe->skhe", score_grad, query_heads, preferred_element_type=jnp.float32
        )
        value_term = jnp.einsum(
            "shqk,sqhe->skhe",
            probs.astype(jnp.bfloat16),
            grad_heads,
            preferred_element_type=jnp.float32,
        )
        block_terms = jnp.concatenate(
            [
                key_term.reshape(1, block_len, model_width),
                value_term.reshape(1, block_len, model_width),
            ],
            axis=-1,
        )
        pair_tally = lax.dynamic_update_slice_in_dim(pair_tally, block_terms, begin, 1)
        return (query_tally, pair_tally)

    tally_start = (
        jnp.zeros((1, tok_count, head_count, head_dim), jnp.float32),
        jnp.zeros((1, total_keys, 2 * model_width), jnp.float32),
    )
    query_tally, pair_tally = lax.fori_loop(0, total_keys // block_len, key_step, tally_start)
    shared = lax.psum_scatter(pair_tally, "ctx", scatter_dimension=1, tiled=True)
    key_grads = (shared[:, :, :model_width] * key_scale).astype(jnp.bfloat16)
    value_grads = shared[:, :, model_width:].astype(jnp.bfloat16)
    query_grads = (query_tally * key_scale).reshape(1, tok_count, model_width).astype(jnp.bfloat16)
    grad_joint = jnp.concatenate([query_grads, key_grads, value_grads], axis=-1).reshape(
        row_count, 3 * model_width
    )
    grad_joint_weight = jnp.einsum(
        "rd,rf->df", flat_tokens, grad_joint, preferred_element_type=jnp.float32
    )
    grad_query_bias = jnp.sum(widen(query_grads).reshape(row_count, model_width), axis=0)
    grad_value_bias = jnp.sum(widen(value_grads).reshape(row_count, model_width), axis=0)
    input_grad = (
        grad_hidden
        + jnp.einsum("rf,df->rd", grad_joint, back_joint, preferred_element_type=jnp.float32)
    ).astype(jnp.bfloat16)
    input_grad = input_grad.reshape(seq_count, tok_count, model_width)
    owned = (
        lax.psum_scatter(grad_joint_weight, ("shard", "ctx"), scatter_dimension=0, tiled=True),
        lax.psum_scatter(grad_query_bias, ("shard", "ctx"), scatter_dimension=0, tiled=True),
        lax.psum_scatter(grad_value_bias, ("shard", "ctx"), scatter_dimension=0, tiled=True),
        lax.psum_scatter(grad_out_weight, ("shard", "ctx"), scatter_dimension=0, tiled=True),
        lax.psum_scatter(grad_out_bias, ("shard", "ctx"), scatter_dimension=0, tiled=True),
        lax.psum_scatter(grad_mid_gain, ("shard", "ctx"), scatter_dimension=0, tiled=True),
        lax.psum_scatter(grad_mid_shift, ("shard", "ctx"), scatter_dimension=0, tiled=True),
        lax.psum_scatter(grad_up_weight, ("shard", "ctx"), scatter_dimension=0, tiled=True),
        lax.psum_scatter(grad_up_bias, ("shard", "ctx"), scatter_dimension=0, tiled=True),
        lax.psum_scatter(grad_down_weight, ("shard", "ctx"), scatter_dimension=0, tiled=True),
        lax.psum_scatter(grad_down_bias, ("shard", "ctx"), scatter_dimension=0, tiled=True),
        lax.psum_scatter(grad_final_gain, ("shard", "ctx"), scatter_dimension=0, tiled=True),
        lax.psum_scatter(grad_final_shift, ("shard", "ctx"), scatter_dimension=0, tiled=True),
    )
    return (
        layer_output,
        input_grad,
        owned[0],
        owned[1],
        owned[2],
        owned[3],
        owned[4],
        owned[5],
        owned[6],
        owned[7],
        owned[8],
        owned[9],
        owned[10],
        owned[11],
        owned[12],
    )


def solution(mesh):
    placed = (
        P("shard", "ctx", None),
        P("shard", "ctx"),
        P(("shard", "ctx"), None),
        P(("shard", "ctx")),
        P(("shard", "ctx")),
        P(("shard", "ctx"), None),
        P(("shard", "ctx")),
        P(("shard", "ctx")),
        P(("shard", "ctx")),
        P(("shard", "ctx"), None),
        P(("shard", "ctx")),
        P(("shard", "ctx"), None),
        P(("shard", "ctx")),
        P(("shard", "ctx")),
        P(("shard", "ctx")),
        P("shard", "ctx", None),
    )
    return jax.shard_map(
        local,
        mesh=mesh,
        in_specs=placed,
        out_specs=(
            P("shard", "ctx", None),
            P("shard", "ctx", None),
            P(("shard", "ctx"), None),
            P(("shard", "ctx")),
            P(("shard", "ctx")),
            P(("shard", "ctx"), None),
            P(("shard", "ctx")),
            P(("shard", "ctx")),
            P(("shard", "ctx")),
            P(("shard", "ctx"), None),
            P(("shard", "ctx")),
            P(("shard", "ctx"), None),
            P(("shard", "ctx")),
            P(("shard", "ctx")),
            P(("shard", "ctx")),
        ),
        check_vma=False,
    )
```

profile of v0, /device:TPU:6, one launch (start us, length us, event | category | flops | bytes accessed | tf_op | source)
XLA Modules:
  0.0 1038.3 jit_solution(8006578424231381487)
XLA Ops:
  16.7 40.8 %all-reduce.19 = (bf16[3072]{0:T(1024)(128)(2,1)S(1)}, bf16[768]{0:T(1024)(128)(2,1)S(1)}, bf16[768]{0:T(1024)(128)(2,1)S(1)}, bf16[768]{0:T(1024)(128)(2,1)S(1)...) all-reduce(bf16[3072]{0:T(1024)(128)(2,1)S(1)} %dynamic-update-slic, ...), channel_id=1, replica_groups=mesh['shard'=4,'ctx'=8] {'shard','ctx'}, use_global_device_ids=true, to_apply=%add.5 | all-reduce | flops 9216 | bytes 36864
  57.5 14.3 %all-gather.7.cloned.1.call-done = bf16[768,2304]{1,0:T(8,128)(2,1)} async-done(((bf16[24,2304]{1,0:T(8,128)(2,1)}), bf16[768,2304]{1,0:T(8,128)(2,1)}) %all-gather.7.cloned.1.call-update) | async-done | bytes 3538960 | tf_op jit(solution)/shard_map/all_gather | solution.py:140
  71.8 2.8 fusion.23
  81.4 17.7 %all_gather.59 = s32[1,1024]{1,0:T(1,128)S(1)} all-gather(s32[1,128]{1,0:T(1,128)S(1)} %copy-done.38), channel_id=1, replica_groups=mesh['shard'=4,'ctx'=8] {'ctx'}, dimensions={1}, use_global_device_ids=true | all-gather | bytes 4608 | tf_op jit(solution)/shard_map/all_gather | solution.py:176
  99.5 19.1 %all-gather.11.cloned.1.call-done = bf16[1,1024,768]{2,1,0:T(8,128)(2,1)} async-done(((bf16[1,128,768]{2,1,0:T(8,128)(2,1)}), bf16[1,1024,768]{2,1,0:T(8,128)(2,1)}) %all-gather.11.cloned.1.call-update) | async-done | bytes 1572880 | tf_op jit(solution)/shard_map/all_gather | solution.py:175
  120.3 43.6 %all-gather.9.cloned.1.call-done = bf16[1,1024,768]{2,1,0:T(8,128)(2,1)} async-done(((bf16[1,128,768]{2,1,0:T(8,128)(2,1)}), bf16[1,1024,768]{2,1,0:T(8,128)(2,1)}) %all-gather.9.cloned.1.call-update) | async-done | bytes 1572880 | tf_op jit(solution)/shard_map/all_gather | solution.py:174
  168.8 3.5 fusion.41
  174.2 45.4 %all-gather.13.cloned.1.call-done = bf16[768,768]{1,0:T(8,128)(2,1)} async-done(((bf16[24,768]{1,0:T(8,128)(2,1)}), bf16[768,768]{1,0:T(8,128)(2,1)}) %all-gather.13.cloned.1.call-update) | async-done | bytes 1179664 | tf_op jit(solution)/shard_map/all_gather | solution.py:143
  222.4 63.1 %all-gather.15.cloned.1.call-done = bf16[768,3072]{1,0:T(8,128)(2,1)} async-done(((bf16[24,3072]{1,0:T(8,128)(2,1)}), bf16[768,3072]{1,0:T(8,128)(2,1)}) %all-gather.15.cloned.1.call-update) | async-done | bytes 4718608 | tf_op jit(solution)/shard_map/all_gather | solution.py:147
  285.5 8.4 multiply_convert_fusion
  293.9 56.8 %all-gather.17.cloned.1.call-done = bf16[3072,768]{1,0:T(8,128)(2,1)} async-done(((bf16[96,768]{1,0:T(8,128)(2,1)}), bf16[3072,768]{1,0:T(8,128)(2,1)}) %all-gather.17.cloned.1.call-update) | async-done | bytes 4718608 | tf_op jit(solution)/shard_map/all_gather | solution.py:149
  350.7 3.7 fusion.85
  356.9 2.5 convert_reduce_fusion
  369.1 3.4 broadcast_in_dim.84
  372.6 29.0 %while.16 = (s32[]{:T(128)}, f32[1,128,12,64]{1,3,2,0:T(8,128)}, f32[1,1024,1536]{1,2,0:T(8,128)}, bf16[1,1024,768]{1,2,0:T(8,128)(2,1)S(1)}, s32[1,128]{1,0:T(1...) while((s32[]{:T(128)}, f32[1,128,12,64]{1,3,2,0:T(8,128)}, ...), condition=%wide.region_12.13_spmd.clone, body=%wide.region_11.12_spmd.clone.sunk | while | flops 512229376 | bytes 116395096 | solution.py:297
  375.3 2.5 fusion.132
  377.7 2.9 fusion.133
  384.4 2.6 copy-done.5
  389.7 2.5 fusion.132
  392.2 2.9 fusion.133
  398.9 2.6 copy-done.5
  405.8 5.2 fusion.78
  412.2 5.0 fusion.70
  418.4 101.0 %reduce-scatter.8.cloned.1.call-done = f32[1,128,1536]{1,2,0:T(8,128)} async-done(((f32[1,1024,1536]{1,2,0:T(8,128)}), f32[1,128,1536]{1,2,0:T(8,128)}) %reduce-scatter.8.cloned.1.call-update) | async-done | bytes 786448 | tf_op jit(solution)/shard_map/reduce_scatter | solution.py:298
  522.1 3.9 convolution_bitcast_fusion.1
  526.0 8.1 copy.72
  536.5 41.3 %all-reduce.18 = (f32[768]{0:T(1024)}, f32[768]{0:T(1024)}, f32[768]{0:T(1024)}, f32[768]{0:T(1024)}, f32[768]{0:T(1024)}, /*index=5*/f32[3072]{0:T(1024)}, f32[768]{0:T(1024)}, f32[768]{0:T(1024)S(1)}, f32[768]{0:T(1024)S(1)}) all-reduce(f32[768]{0:T(1024)} %reduce_sum.190, ...), channel_id=4, replica_groups=mesh['shard'=4,'ctx'=8] {'shard','ctx'}, use_global_device_ids=true, to_apply=%region_16.17.clone | all-reduce | flops 9216 | bytes 73728
  587.8 3.2 fusion.45
  591.1 33.1 %reduce-scatter.10.cloned.1.call-done = f32[24,768]{1,0:T(8,128)} async-done(((f32[768,768]{1,0:T(8,128)}), f32[24,768]{1,0:T(8,128)}) %reduce-scatter.10.cloned.1.call-update) | async-done | bytes 73744 | tf_op jit(solution)/shard_map/reduce_scatter | solution.py:319
  624.2 141.3 %reduce-scatter.12.cloned.1.call-done = f32[24,3072]{1,0:T(8,128)} async-done(((f32[768,3072]{1,0:T(8,128)}), f32[24,3072]{1,0:T(8,128)}) %reduce-scatter.12.cloned.1.call-update) | async-done | bytes 294928 | tf_op jit(solution)/shard_map/reduce_scatter | solution.py:323
  765.5 141.5 %reduce-scatter.14.cloned.1.call-done = f32[96,768]{1,0:T(8,128)} async-done(((f32[3072,768]{1,0:T(8,128)}), f32[96,768]{1,0:T(8,128)}) %reduce-scatter.14.cloned.1.call-update) | async-done | bytes 294928 | tf_op jit(solution)/shard_map/reduce_scatter | solution.py:325
  906.9 124.8 %reduce-scatter.16.cloned.1.call-done = f32[24,2304]{1,0:T(8,128)} async-done(((f32[768,2304]{1,0:T(8,128)}), f32[24,2304]{1,0:T(8,128)}) %reduce-scatter.16.cloned.1.call-update) | async-done | bytes 221200
  (257 shorter events, 74.3 us)
Async XLA Ops:
  7.2 64.6 %all-gather.7.cloned.1.call-start = ((), (), s32[]{:S(2)}) async-start(), calls=%async_computation.5 | async-start | bytes 3649536 | tf_op jit(solution)/shard_map/all_gather | solution.py:140
  8.8 109.7 %all-gather.11.cloned.1.call-start = ((), (), s32[]{:S(2)}) async-start(), calls=%async_computation.7 | async-start | bytes 1769472 | tf_op jit(solution)/shard_map/all_gather | solution.py:175
  74.6 6.8 copy-start.38
  75.4 88.5 %all-gather.9.cloned.1.call-start = ((), (), s32[]{:S(2)}) async-start(), calls=%async_computation.6 | async-start | bytes 1769472 | tf_op jit(solution)/shard_map/all_gather | solution.py:174
  76.2 143.4 %all-gather.13.cloned.1.call-start = ((), (), s32[]{:S(2)}) async-start(), calls=%async_computation.8 | async-start | bytes 1216512 | tf_op jit(solution)/shard_map/all_gather | solution.py:143
  76.9 208.6 %all-gather.15.cloned.1.call-start = ((), (), s32[]{:S(2)}) async-start(), calls=%async_computation.9 | async-start | bytes 4866048 | tf_op jit(solution)/shard_map/all_gather | solution.py:147
  77.6 273.1 %all-gather.17.cloned.1.call-start = ((), (), s32[]{:S(2)}) async-start(), calls=%async_computation.10 | async-start | bytes 4866048 | tf_op jit(solution)/shard_map/all_gather | solution.py:149
  78.4 441.0 %reduce-scatter.8.cloned.1.call-start = ((), (), s32[]{:S(2)}) async-start(), calls=%async_computation.11 | async-start | bytes 7077888 | tf_op jit(solution)/shard_map/reduce_scatter | solution.py:298
  99.1 21.2 %copy-start.34 = (s32[1,1024]{1,0:T(1,128)}, s32[1,1024]{1,0:T(1,128)S(1)}, u32[]{:S(2)}) copy-start(s32[1,1024]{1,0:T(1,128)S(1)} %all_gather.59) | copy-start | bytes 12292
  99.3 67.6 %copy-start.28 = (pred[128,1024]{1,0:T(8,128)(4,1)}, pred[128,1024]{1,0:T(8,128)(4,1)S(1)}, u32[]{:S(2)}) copy-start(pred[128,1024]{1,0:T(8,128)(4,1)S(1)} %broadcast_compare_fusion.1) | copy-start | bytes 393220
  168.8 50.8 %copy-start.24 = (bf16[1,128,768]{2,1,0:T(8,128)(2,1)S(1)}, bf16[1,128,768]{2,1,0:T(8,128)(2,1)}, u32[]{:S(2)}) copy-start(bf16[1,128,768]{2,1,0:T(8,128)(2,1)} %param.18) | copy-start | bytes 589828
  221.4 140.4 %copy-start.40 = (f32[128]{0:T(128)}, f32[128]{0:T(128)S(1)}, u32[]{:S(2)}) copy-start(f32[128]{0:T(128)S(1)} %broadcast_multiply_fusion.5) | copy-start | bytes 1540
  222.4 139.4 %copy-start.46 = (f32[128]{0:T(128)}, f32[128]{0:T(128)S(1)}, u32[]{:S(2)}) copy-start(f32[128]{0:T(128)S(1)} %add_rsqrt_fusion.1) | copy-start | bytes 1540
  222.4 128.3 %copy-start.43 = (f32[768]{0:T(1024)S(1)}, f32[768]{0:T(1024)}, u32[]{:S(2)}) copy-start(f32[768]{0:T(1024)} %convert_element_type.203) | copy-start | bytes 9220
  350.7 6.2 slice-start
  350.7 3.9 copy-start.26
  350.7 3.9 copy-start.37
  350.7 4.7 copy-start.42
  350.7 6.2 slice-start.1
  350.7 6.2 copy-start.50
  355.4 4.0 slice-start.2
  359.4 3.2 copy-start.27
  380.6 3.3 copy-start.4
  383.9 3.1 copy-start.7
  395.1 3.3 copy-start.4
  401.6 222.6 %reduce-scatter.10.cloned.1.call-start = ((), (), s32[]{:S(2)}) async-start(), calls=%async_computation.12 | async-start | bytes 2433024 | tf_op jit(solution)/shard_map/reduce_scatter | solution.py:319
  404.5 360.9 %reduce-scatter.12.cloned.1.call-start = ((), (), s32[]{:S(2)}) async-start(), calls=%async_computation.13 | async-start | bytes 9732096 | tf_op jit(solution)/shard_map/reduce_scatter | solution.py:323
  411.0 495.9 %reduce-scatter.14.cloned.1.call-start = ((), (), s32[]{:S(2)}) async-start(), calls=%async_computation.14 | async-start | bytes 9732096 | tf_op jit(solution)/shard_map/reduce_scatter | solution.py:325
  417.3 104.8 %copy-start.25 = (bf16[1,128,768]{2,1,0:T(8,128)(2,1)S(1)}, bf16[1,128,768]{2,1,0:T(8,128)(2,1)}, u32[]{:S(2)}) copy-start(bf16[1,128,768]{2,1,0:T(8,128)(2,1)} %param.18) | copy-start | bytes 589828
  417.3 614.5 %reduce-scatter.16.cloned.1.call-start = ((), (), s32[]{:S(2)}) async-start(), calls=%async_computation.15 | async-start | bytes 7299072
  418.4 107.6 %copy-start.29 = (bf16[1,128,12,64]{1,3,2,0:T(8,128)(2,1)}, bf16[1,128,12,64]{1,3,2,0:T(8,128)(2,1)S(1)}, u32[]{:S(2)}) copy-start(bf16[1,128,12,64]{1,3,2,0:T(8,128)(2,1)S(1)} %get-tuple-element.370) | copy-start | bytes 589828
  534.1 53.8 %copy-start.17 = (bf16[768,2304]{1,0:T(8,128)(2,1)S(1)}, bf16[768,2304]{1,0:T(8,128)(2,1)}, u32[]{:S(2)}) copy-start(bf16[768,2304]{1,0:T(8,128)(2,1)} %all-gather.7.cloned.1.call-done) | copy-start | bytes 10616836
  (47 other events, 81.4 us)
Sparse Core Ops, SparseCore 0:
  11.5 60.2 all-gather.6
  75.6 42.9 all-gather.10
  121.3 42.5 all-gather.8
  167.2 52.3 all-gather.12
  222.9 62.5 all-gather.14
  288.8 61.8 all-gather.16
  401.7 117.6 reduce-scatter.7
  525.3 98.8 reduce-scatter.9
  630.7 134.7 reduce-scatter.11
  771.8 135.0 reduce-scatter.13
  913.2 118.5 reduce-scatter.15
where the time goes:
time: 1040 us
  waiting for transfers between devices  785 us (75%)
  blocking collectives  99.8 us (10%)
  matrix products  62.1 us (6%)
  local copies, waits for them, and re-layouts  52.2 us (5%)
  other arithmetic  24.5 us (2%)
  between operations  14.4 us (1%)
    reduce_scatter x1, waiting for transfers between devices, local(): lax.psum_scatter(grad_down_weight, ('shard', 'ctx'), scatter_dimension=0,...  141 us
    reduce_scatter x1, waiting for transfers between devices, local(): lax.psum_scatter(grad_up_weight, ('shard', 'ctx'), scatter_dimension=0, t...  141 us
    unnamed x12, waiting for transfers between devices  126 us
    reduce_scatter x1, waiting for transfers between devices, local(): lax.psum_scatter(pair_tally, 'ctx', scatter_dimension=1, tiled=True)  101 us
    unnamed x2, blocking collectives  82.1 us
    all_gather x1, waiting for transfers between devices, local(): lax.all_gather(halve(up_weight), ('shard', 'ctx'), axis=0, tiled=True)  63.1 us
    all_gather x1, waiting for transfers between devices, local(): lax.all_gather(halve(down_weight), ('shard', 'ctx'), axis=0, tiled=True)  56.8 us
    all_gather x1, waiting for transfers between devices, local(): lax.all_gather(halve(out_weight), ('shard', 'ctx'), axis=0, tiled=True)  45.4 us
  transfers between devices with their start and end apart: 11, of which 11 were waited for; matrix products, arithmetic and copies ran while one was open for 7% of the time, Pallas kernels for 0%

commit v1 on v0

v1 whole, which is shorter than its diff:
```python
import functools

import jax
import jax.numpy as jnp
from jax import lax
from jax.experimental import pallas as pl
from jax.experimental.pallas import tpu as pltpu
from jax.sharding import PartitionSpec as P

HEADS = 12
MASKED = -1e30
EPSILON = 1e-05
BF = jnp.bfloat16
F32 = jnp.float32
EXTRA = 64
PAD = 16
AXES = ("shard", "ctx")


def dot(a, b, dims=((1,), (0,))):
    return lax.dot_general(a, b, (dims, ((), ())), preferred_element_type=F32)


def normalize_fwd(hidden, gain, shift):
    center = hidden - jnp.mean(hidden, axis=-1, keepdims=True)
    inverse_dev = lax.rsqrt(jnp.mean(center * center, axis=-1, keepdims=True) + EPSILON)
    normed = center * inverse_dev
    return normed * gain + shift, normed, inverse_dev


def normalize_back(upstream, normed, inverse_dev, gain):
    scaled = upstream * gain
    inner = (
        scaled
        - jnp.mean(scaled, axis=-1, keepdims=True)
        - normed * jnp.mean(scaled * normed, axis=-1, keepdims=True)
    )
    return inner * inverse_dev, jnp.sum(upstream * normed, axis=0), jnp.sum(upstream, axis=0)


def key_chunk(total):
    return total if total <= 1024 else 1024


def attn_fwd_kernel(heads, dim, block, q_ref, kv_ref, segq_ref, segk_ref, o_ref, lse_ref, segb):
    total = kv_ref.shape[0]
    width = heads * dim
    chunk = key_chunk(total)
    steps = total // chunk
    segb[...] = jnp.broadcast_to(segk_ref[...], segb.shape)
    scale = dim ** (-0.5)

    def scores(h, n, qh, begin):
        kh = kv_ref[pl.ds(begin, chunk), h * dim : (h + 1) * dim]
        s = dot(kh, qh, ((1,), (1,)))
        same = segb[pl.ds(begin, chunk), :] == segq_ref[n]
        return jnp.where(same, s, MASKED)

    for h in range(heads):
        vcols = slice(width + h * dim, width + (h + 1) * dim)

        def query_step(n, _, h=h, vcols=vcols):
            rows = pl.ds(pl.multiple_of(n * block, block), block)
            qh = q_ref[rows, h * dim : (h + 1) * dim] * jnp.asarray(scale, BF)
            if steps == 1:
                s = scores(h, n, qh, 0)
                m = jnp.max(s, axis=0, keepdims=True)
                p = jnp.exp(s - m)
                l = jnp.sum(p, axis=0, keepdims=True)
                acc = dot(kv_ref[:, vcols], p.astype(BF), ((0,), (0,)))
            else:

                def chunk_step(i, carry):
                    m0, l0, acc0 = carry
                    begin = pl.multiple_of(i * chunk, chunk)
                    s = scores(h, n, qh, begin)
                    m1 = jnp.maximum(m0, jnp.max(s, axis=0, keepdims=True))
                    p = jnp.exp(s - m1)
                    f = jnp.exp(m0 - m1)
                    l1 = l0 * f + jnp.sum(p, axis=0, keepdims=True)
                    part = dot(kv_ref[pl.ds(begin, chunk), vcols], p.astype(BF), ((0,), (0,)))
                    return m1, l1, acc0 * f + part

                start = (
                    jnp.full((1, block), MASKED, F32),
                    jnp.zeros((1, block), F32),
                    jnp.zeros((dim, block), F32),
                )
                m, l, acc = lax.fori_loop(0, steps, chunk_step, start)
            o_ref[rows, h * dim : (h + 1) * dim] = jnp.transpose(acc / l).astype(BF)
            lse_ref[h, n] = m + jnp.log(l)
            return 0

        lax.fori_loop(0, q_ref.shape[0] // block, query_step, 0)


def attn_bwd_kernel(
    heads, dim, block, q_ref, kv_ref, segq_ref, segk_ref, lse_ref, o_ref, gm_ref, dq_ref, dkv_ref,
    segb, dk_acc, dv_acc,
):
    total = kv_ref.shape[0]
    width = heads * dim
    chunk = key_chunk(total)
    steps = total // chunk
    segb[...] = jnp.broadcast_to(segk_ref[...], segb.shape)
    scale = dim ** (-0.5)
    for h in range(heads):
        cols = slice(h * dim, (h + 1) * dim)
        vcols = slice(width + h * dim, width + (h + 1) * dim)
        dk_acc[...] = jnp.zeros_like(dk_acc)
        dv_acc[...] = jnp.zeros_like(dv_acc)

        def query_step(n, _, h=h, cols=cols, vcols=vcols):
            rows = pl.ds(pl.multiple_of(n * block, block), block)
            qh = q_ref[rows, cols] * jnp.asarray(scale, BF)
            gm = gm_ref[rows, cols]
            prod = gm.astype(F32) * o_ref[rows, cols].astype(F32)
            delta = jnp.sum(jnp.transpose(prod), axis=0, keepdims=True)
            lse = lse_ref[h, n]
            segq = segq_ref[n]

            def part(begin):
                ks = pl.ds(begin, chunk)
                kh = kv_ref[ks, cols]
                s = dot(kh, qh, ((1,), (1,)))
                s = jnp.where(segb[ks, :] == segq, s, MASKED)
                p = jnp.exp(s - lse)
                dp = dot(kv_ref[ks, vcols], gm, ((1,), (1,)))
                ds = (p * (dp - delta)).astype(BF)
                dk_acc[ks, :] += dot(ds, qh)
                dv_acc[ks, :] += dot(p.astype(BF), gm)
                return dot(kh, ds, ((0,), (0,)))

            if steps == 1:
                dqt = part(0)
            else:
                dqt = lax.fori_loop(
                    0,
                    steps,
                    lambda i, acc: acc + part(pl.multiple_of(i * chunk, chunk)),
                    jnp.zeros((dim, block), F32),
                )
            dq_ref[rows, cols] = (jnp.transpose(dqt) * scale).astype(BF)
            return 0

        lax.fori_loop(0, q_ref.shape[0] // block, query_step, 0)
        dkv_ref[:, cols] = dk_acc[...].astype(BF)
        dkv_ref[:, vcols] = dv_acc[...].astype(BF)


def attend(q, kv, segq, segk, heads, dim, block):
    total, rows = kv.shape[0], q.shape[0]
    return pl.pallas_call(
        functools.partial(attn_fwd_kernel, heads, dim, block),
        out_shape=(
            jax.ShapeDtypeStruct((rows, heads * dim), BF),
            jax.ShapeDtypeStruct((heads, rows // block, 1, block), F32),
        ),
        scratch_shapes=[pltpu.VMEM((total, block), F32)],
        name="attend",
    )(q, kv, segq, segk)


def attend_back(q, kv, segq, segk, lse, mixed, gm, heads, dim, block):
    total, rows = kv.shape[0], q.shape[0]
    return pl.pallas_call(
        functools.partial(attn_bwd_kernel, heads, dim, block),
        out_shape=(
            jax.ShapeDtypeStruct((rows, heads * dim), BF),
            jax.ShapeDtypeStruct((total, 2 * heads * dim), BF),
        ),
        scratch_shapes=[
            pltpu.VMEM((total, block), F32),
            pltpu.VMEM((total, dim), F32),
            pltpu.VMEM((total, dim), F32),
        ],
        name="attend_back",
    )(q, kv, segq, segk, lse, mixed, gm)


def place_kernel(count, index_ref, *refs):
    out_ref = refs[count]
    own = index_ref[0]
    for r in range(count):
        out_ref[own ^ r] = refs[r][...]


def place(blocks, index):
    count = len(blocks)
    spec = pl.BlockSpec(memory_space=pltpu.VMEM)
    return pl.pallas_call(
        functools.partial(place_kernel, count),
        out_shape=jax.ShapeDtypeStruct((count,) + blocks[0].shape, blocks[0].dtype),
        in_specs=[pl.BlockSpec(memory_space=pltpu.SMEM)] + [spec] * count,
        out_specs=spec,
        name="place",
    )(index.reshape(1).astype(jnp.int32), *blocks)


def unplace_kernel(count, index_ref, in_ref, *out_refs):
    own = index_ref[0]
    for r in range(count):
        out_refs[r][...] = in_ref[own ^ r]


def unplace(stacked, index):
    count = stacked.shape[0]
    spec = pl.BlockSpec(memory_space=pltpu.VMEM)
    return pl.pallas_call(
        functools.partial(unplace_kernel, count),
        out_shape=[jax.ShapeDtypeStruct(stacked.shape[1:], stacked.dtype)] * count,
        in_specs=[pl.BlockSpec(memory_space=pltpu.SMEM), spec],
        out_specs=[spec] * count,
        name="unplace",
    )(index.reshape(1).astype(jnp.int32), stacked)


def build(shards, ctxs):
    group = ctxs // shards
    custom = group == 2

    def permute(x, where):
        pairs = []
        for s in range(shards):
            for c in range(ctxs):
                s2, a2, b2 = where(s, c // group, c % group)
                pairs.append((s * ctxs + c, s2 * ctxs + a2 * group + b2))
        return lax.ppermute(x, AXES, pairs)

    def swap_plane(x):
        return permute(x, lambda s, a, b: (a, s, b))

    def over_shard(x, k):
        return permute(x, lambda s, a, b: (s ^ k, a, b))

    def over_b(x, j):
        return permute(x, lambda s, a, b: (s, a, b ^ j))

    def over_a(x, i):
        return permute(x, lambda s, a, b: (s, a ^ i, b))

    def gather_shard(x):
        r2 = over_shard(x, 2)
        r1 = over_shard(x, 1)
        r3 = over_shard(r2, 1)
        return [x, r2, r1, r3]

    def scatter_shard(p):
        rows = p.shape[0] // 4
        r = over_shard(p[2 * rows :].astype(BF), 1).astype(F32)
        sent = (p[rows : 2 * rows] + r[rows:]).astype(BF)
        return p[:rows] + r[:rows] + over_shard(sent, 2).astype(F32)

    def gather_ctx(x, index):
        if not custom:
            return lax.all_gather(x, "ctx", axis=0, tiled=False)
        firsts = [x] + [over_a(x, i) for i in range(1, shards)]
        blocks = []
        for f in firsts:
            blocks += [f, over_b(f, 1)]
        return place(blocks, index)

    def scatter_ctx(y, index):
        if not custom:
            return lax.psum_scatter(y, "ctx", scatter_dimension=0, tiled=False).astype(F32)
        rel = unplace(y, index)
        sums = [
            rel[2 * i].astype(F32) + over_b(rel[2 * i + 1], 1).astype(F32) for i in range(shards)
        ]
        total = sums[0]
        for i in range(1, shards):
            total = total + over_a(sums[i].astype(BF), i).astype(F32)
        return total

    def local(
        tokens, segments, joint_weight, query_bias, value_bias, out_weight, out_bias, mid_gain,
        mid_shift, up_weight, up_bias, down_weight, down_bias, final_gain, final_shift, cotangent,
    ):
        _, toks, width = tokens.shape
        rows = joint_weight.shape[0]
        ff_rows = down_weight.shape[0]
        ff_part = up_weight.shape[1] // shards
        per = ff_rows // rows
        heads = HEADS // shards
        dim = width // HEADS
        hw = heads * dim
        own_s = lax.axis_index("shard")
        own_c = lax.axis_index("ctx")

        joint = joint_weight.astype(BF).reshape(rows, 3, shards, hw)
        joint = jnp.transpose(joint, (2, 0, 1, 3)).reshape(shards, rows, 3 * hw)
        small = [query_bias, value_bias, out_bias, mid_gain, mid_shift, down_bias, final_gain, final_shift]
        small = jnp.concatenate(
            [jnp.stack(small, axis=1), up_bias.reshape(rows, per)], axis=1
        ).astype(BF)
        small = jnp.pad(small, ((0, 0), (0, EXTRA - small.shape[1])))
        small = jnp.broadcast_to(small[None], (shards, rows, EXTRA))
        up = jnp.transpose(up_weight.astype(BF).reshape(rows, shards, ff_part), (1, 0, 2))
        payload = jnp.concatenate([joint, small, up], axis=2)
        payload = lax.all_to_all(payload, "shard", 0, 0, tiled=True)
        jw = 3 * hw + EXTRA
        seg_rows = jnp.pad(segments.astype(BF), ((0, PAD - 1), (0, width - toks)))
        mine = swap_plane(jnp.concatenate([tokens[0], seg_rows], axis=0))
        cot = swap_plane(cotangent[0]).astype(F32)
        blocks = []
        for j in range(group):
            blocks += gather_shard(mine if j == 0 else over_b(mine, j))
        table = gather_ctx(payload[:, :, :jw], own_c)
        table = jnp.transpose(table, (1, 0, 2, 3)).reshape(width, jw)
        bulk = jnp.concatenate(
            [
                out_weight.astype(BF),
                down_weight.astype(BF),
                payload[:, :, jw:].reshape(shards * rows, ff_part),
            ],
            axis=0,
        )
        bulk = gather_ctx(bulk, own_c)
        w_out = bulk[:, :rows].reshape(ctxs * rows, width)
        w_down = bulk[:, rows : rows + ff_rows].reshape(ctxs * ff_rows, width)
        w_up = bulk[:, rows + ff_rows :].reshape(ctxs, shards, rows, ff_part)
        w_up = jnp.transpose(w_up, (1, 0, 2, 3)).reshape(width, ff_part)

        w_joint = table[:, : 3 * hw]
        vectors = jnp.transpose(table[:, 3 * hw :].astype(F32))
        out_b, mid_g, mid_s, down_b, final_g, final_s = (vectors[i][None] for i in range(2, 8))
        quarter = lax.dynamic_slice_in_dim(vectors, own_s * hw, hw, 1)
        query_b, value_b = quarter[0], quarter[1]
        up_b = jnp.transpose(
            lax.dynamic_slice_in_dim(vectors, own_s * (width // shards), width // shards, 1)[8 : 8 + per]
        ).reshape(ff_part)
        joint_b = jnp.concatenate([query_b, jnp.zeros((hw,), F32), value_b])

        x_all = jnp.concatenate([b[:toks] for b in blocks], axis=0)
        seg_all = jnp.stack([b[toks, :toks] for b in blocks], axis=0).astype(F32)
        x_own = mine[:toks].astype(F32)
        projected = (dot(x_all, w_joint) + joint_b).astype(BF)
        wide = shards * toks
        q = projected[:wide, :hw]
        kv = projected[:, hw:]
        segq = seg_all[:shards].reshape(shards, 1, toks)
        segk = seg_all.reshape(-1, 1)
        mixed, lse = attend(q, kv, segq, segk, heads, dim, toks)
        attn = scatter_shard(dot(mixed, w_out))
        mid, mid_n, mid_r = normalize_fwd(x_own + attn + out_b, mid_g, mid_s)

        mids = jnp.concatenate(gather_shard(mid.astype(BF)), axis=0)
        up_value = dot(mids, w_up) + up_b
        act, gate_back = jax.vjp(lambda v: jax.nn.gelu(v, approximate=False), up_value)
        act = act.astype(BF)
        ffn = scatter_shard(dot(act, w_down))
        final, final_n, final_r = normalize_fwd(mid + ffn + down_b, final_g, final_s)
        layer_output = swap_plane(final.astype(BF))[None]

        g_y, g_final_gain, g_final_shift = normalize_back(cot, final_n, final_r, final_g)
        g_f = g_y.astype(BF)
        g_down_bias = jnp.sum(g_f.astype(F32), axis=0)
        g_fs = jnp.concatenate(gather_shard(g_f), axis=0)
        g_act = dot(g_fs, w_down, ((1,), (1,)))
        g_u = gate_back(g_act)[0].astype(BF)
        g_mid = g_y + scatter_shard(dot(g_u, w_up, ((1,), (1,))))
        g_down = dot(act, g_fs, ((0,), (0,)))
        g_up = dot(mids, g_u, ((0,), (0,)))
        g_up_bias = jnp.sum(g_u.astype(F32), axis=0)
        g_h, g_mid_gain, g_mid_shift = normalize_back(g_mid, mid_n, mid_r, mid_g)
        g_a = g_h.astype(BF)
        g_out_bias = jnp.sum(g_a.astype(F32), axis=0)
        g_as = jnp.concatenate(gather_shard(g_a), axis=0)
        g_m = dot(g_as, w_out, ((1,), (1,))).astype(BF)
        g_out = dot(mixed, g_as, ((0,), (0,)))

        bulk_grad = jnp.concatenate(
            [
                g_out.astype(BF).reshape(ctxs, rows, width),
                g_down.astype(BF).reshape(ctxs, ff_rows, width),
                jnp.transpose(g_up.astype(BF).reshape(shards, ctxs, rows, ff_part), (1, 0, 2, 3)).reshape(
                    ctxs, shards * rows, ff_part
                ),
            ],
            axis=1,
        )
        bulk_grad = scatter_ctx(bulk_grad, own_c)

        dq, dkv = attend_back(q, kv, segq, segk, lse, mixed, g_m, heads, dim, toks)
        g_joint = jnp.concatenate(
            [dot(x_all[:wide], dq, ((0,), (0,))), dot(x_all, dkv, ((0,), (0,)))], axis=1
        )
        dkv_own = dkv[:wide].astype(F32)
        for j in range(1, group):
            dkv_own = dkv_own + over_b(dkv[j * wide : (j + 1) * wide], j).astype(F32)
        g_qkv = jnp.concatenate([dq, dkv_own.astype(BF)], axis=1)
        g_in = scatter_shard(dot(g_qkv, w_joint, ((1,), (1,))))
        input_grad = swap_plane((g_h + g_in).astype(BF))[None]

        g_query_bias = jnp.sum(dq.astype(F32), axis=0)
        g_value_bias = jnp.sum(dkv[:, hw:].astype(F32), axis=0)

        def spread(v):
            return lax.dynamic_update_slice_in_dim(
                jnp.zeros((width,) + v.shape[1:], F32), v, own_s * v.shape[0], 0
            )

        columns = jnp.stack(
            [
                spread(g_query_bias), spread(g_value_bias), g_out_bias, g_mid_gain, g_mid_shift,
                g_down_bias, g_final_gain, g_final_shift,
            ],
            axis=1,
        )
        columns = jnp.concatenate([columns, spread(g_up_bias.reshape(width // shards, per))], axis=1)
        columns = jnp.pad(columns, ((0, 0), (0, EXTRA - columns.shape[1])))
        g_table = jnp.concatenate([g_joint, columns], axis=1).astype(BF)
        g_table = jnp.transpose(g_table.reshape(shards, ctxs, rows, jw), (1, 0, 2, 3))
        g_table = scatter_ctx(g_table, own_c)
        payload = jnp.concatenate(
            [g_table, bulk_grad[rows + ff_rows :].reshape(shards, rows, ff_part)], axis=2
        ).astype(BF)
        payload = lax.all_to_all(payload, "shard", 0, 0, tiled=True).astype(F32)
        g_joint_weight = jnp.transpose(
            payload[:, :, : 3 * hw].reshape(shards, rows, 3, hw), (1, 2, 0, 3)
        ).reshape(rows, 3 * width)
        g_up_weight = jnp.transpose(payload[:, :, jw:], (1, 0, 2)).reshape(rows, shards * ff_part)
        sums = jnp.sum(payload[:, :, 3 * hw : jw], axis=0)
        return (
            layer_output,
            input_grad,
            g_joint_weight,
            sums[:, 0],
            sums[:, 1],
            bulk_grad[:rows],
            sums[:, 2],
            sums[:, 3],
            sums[:, 4],
            g_up_weight,
            sums[:, 8 : 8 + per].reshape(ff_rows),
            bulk_grad[rows : rows + ff_rows],
            sums[:, 5],
            sums[:, 6],
            sums[:, 7],
        )

    return local


def solution(mesh):
    both = P(AXES)
    mat = P(AXES, None)
    act = P("shard", "ctx", None)
    return jax.shard_map(
        build(mesh.shape["shard"], mesh.shape["ctx"]),
        mesh=mesh,
        in_specs=(
            act, P("shard", "ctx"), mat, both, both, mat, both, both, both, mat, both, mat, both,
            both, both, act,
        ),
        out_specs=(
            act, act, mat, both, both, mat, both, both, both, mat, both, mat, both, both, both,
        ),
        check_vma=False,
    )
```

time: 1040 us -> 310 us (0.30)
  waiting for transfers between devices: 785 us -> 136 us
  blocking collectives: 99.8 us -> 0 us
  starting transfers between devices: 0.45 us -> 64 us
  matrix products: 62.1 us -> 23.4 us
  Pallas kernels: 0 us -> 32.4 us
  local copies, waits for them, and re-layouts: 52.2 us -> 33.6 us
  between operations: 14.4 us -> 2.07 us
    reduce_scatter x4 -> x0, waiting for transfers between devices: 417 us -> none  [the longest x1 141 us: local(): lax.psum_scatter(grad_down_weight, ('shard', 'ctx'), scatter_dimension=0,...]
    all_gather x6 -> x0, waiting for transfers between devices: 242 us -> none  [the longest x1 63.1 us: local(): lax.all_gather(halve(up_weight), ('shard', 'ctx'), axis=0, tiled=True)]
    ppermute x0 -> x57, waiting for transfers between devices: none -> 132 us  [permute(): return lax.ppermute(x, AXES, pairs)]
    unnamed x12 -> x0, waiting for transfers between devices: 126 us -> none
    unnamed x2 -> x0, blocking collectives: 82.1 us -> none
    ppermute x0 -> x57, starting transfers between devices: none -> 56.6 us  [permute(): return lax.ppermute(x, AXES, pairs)]
    dot_general x24 -> x13, matrix products: 62.1 us -> 23.4 us  [dot(): return lax.dot_general(a, b, (dims, ((), ())), preferred_element_type=F32)]
    pallas_call x0 -> x6, Pallas kernels: none -> 32.4 us  [the longest x1 10.8 us: attend_back(): pl.pallas_call(functools.partial(attn_bwd_kernel, heads, dim, block), out...]
  transfers between devices with their start and end apart: 11 -> 59, of which waited for: 11 -> 33; matrix products, arithmetic and copies ran while one was open for 7% -> 14% of each run, Pallas kernels for 0% -> 7%
where the time goes in v1:
time: 310 us; the launch traced here: 309 us
  waiting for transfers between devices  136 us (44%)
  starting transfers between devices  64 us (21%)
  local copies, waits for them, and re-layouts  33.6 us (11%)
  Pallas kernels  32.4 us (10%)
  matrix products  23.4 us (8%)
  other arithmetic  17.6 us (6%)
    ppermute x57, waiting for transfers between devices, permute(): return lax.ppermute(x, AXES, pairs)  132 us
    ppermute x57, starting transfers between devices, permute(): return lax.ppermute(x, AXES, pairs)  56.6 us
    dot_general x13, matrix products, dot(): return lax.dot_general(a, b, (dims, ((), ())), preferred_element_type=F32)  23.4 us
    pallas_call x1, Pallas kernels, attend_back(): pl.pallas_call(functools.partial(attn_bwd_kernel, heads, dim, block), out...  10.8 us
    pallas_call x1, Pallas kernels, attend(): pl.pallas_call(functools.partial(attn_fwd_kernel, heads, dim, block), out...  10.3 us
    unnamed x156, local copies, waits for them, and re-layouts  9 us
  transfers between devices with their start and end apart: 59, of which 33 were waited for; matrix products, arithmetic and copies ran while one was open for 14% of the time, Pallas kernels for 7%

profile of v1, /device:TPU:6, one launch (start us, length us, event | category | flops | bytes accessed | tf_op | source)
XLA Modules:
  0.0 308.7 jit_solution(13504472801429937521)
XLA Ops:
  5.2 4.0 %all-to-all-start = ((bf16[4,24,1408]{2,1,0:T(8,128)(2,1)}), bf16[4,24,1408]{2,1,0:T(8,128)(2,1)S(1)}, u32[]{:S(2)}, u32[]{:S(2)}) async-start(bf16[4,24,1408]{2,1,0:T(8,128)(2,1)} %concatenate.60), calls=%async_computation | async-start | bytes 540672 | tf_op jit(solution)/shard_map/all_to_all | solution.py:300
  9.2 4.0 %collective-permute-start = (bf16[144,768]{1,0:T(8,128)(2,1)S(1)}, bf16[144,768]{1,0:T(8,128)(2,1)S(1)}, u32[]{:S(2)}, u32[]{:S(2)}) collective-permute-start(bf16[144,768]{1,0:T(8,128)(2,1)S(1)} %fusion.43), channel_id=1, source_target_pairs={{0,0},{1,1},{2,8},{3,9},{4,16},{5,17},{6,24},{7,25},{8,2},{9,3},{1... | collective-permute-start | bytes 663560 | tf_op jit(solution)/shard_map/ppermute | solution.py:228
  18.1 13.0 %collective-permute-done = bf16[144,768]{1,0:T(8,128)(2,1)S(1)} collective-permute-done((bf16[144,768]{1,0:T(8,128)(2,1)S(1)}, bf16[144,768]{1,0:T(8,128)(2,1)S(1)}, u32[]{:S(2)}, u32[]{:S(2)}) %collective-permute-start) | collective-permute-done | bytes 221216 | tf_op jit(solution)/shard_map/ppermute | solution.py:228
  31.9 5.3 %collective-permute-done.1 = bf16[144,768]{1,0:T(8,128)(2,1)} collective-permute-done((bf16[144,768]{1,0:T(8,128)(2,1)S(1)}, bf16[144,768]{1,0:T(8,128)(2,1)}, u32[]{:S(2)}, u32[]{:S(2)}) %collective-permute-start.1) | collective-permute-done | bytes 221216 | tf_op jit(solution)/shard_map/ppermute | solution.py:228
  60.1 10.4 %collective-permute-done.18.refs_4_ = bf16[216,768]{1,0:T(8,128)(2,1)S(1)} collective-permute-done((bf16[216,768]{1,0:T(8,128)(2,1)S(1)}, bf16[216,768]{1,0:T(8,128)(2,1)S(1)}, u32[]{:S(2)}, u32[]{:S(2)}) %collective-permute-start.18) | collective-permute-done | bytes 331808 | tf_op jit(solution)/shard_map/ppermute | solution.py:228
  76.6 4.5 %collective-permute-done.17.refs_3_ = bf16[216,768]{1,0:T(8,128)(2,1)S(1)} collective-permute-done((bf16[216,768]{1,0:T(8,128)(2,1)S(1)}, bf16[216,768]{1,0:T(8,128)(2,1)S(1)}, u32[]{:S(2)}, u32[]{:S(2)}) %collective-permute-start.17) | collective-permute-done | bytes 331808 | tf_op jit(solution)/shard_map/ppermute | solution.py:228
  81.2 6.7 %collective-permute-done.19.refs_5_ = bf16[216,768]{1,0:T(8,128)(2,1)S(1)} collective-permute-done((bf16[216,768]{1,0:T(8,128)(2,1)S(1)}, bf16[216,768]{1,0:T(8,128)(2,1)S(1)}, u32[]{:S(2)}, u32[]{:S(2)}) %collective-permute-start.19) | collective-permute-done | bytes 331808 | tf_op jit(solution)/shard_map/ppermute | solution.py:228
  88.6 2.9 collective-permute-done.21.refs_7_
  91.6 3.3 %place.3 = bf16[8,216,768]{2,1,0:T(8,128)(2,1)} custom-call(s32[1]{0:T(128)} %bitcast.1.index_ref, bf16[216,768]{1,0:T(8,128)(2,1)} %copy-done.4, bf16[216,768]{1,0:T(8,128)(2,1)} %collective-permute-done.15.refs_1_, bf16[216,768]{1,0:T(8,128)(2,1)} %copy-done.16, bf16[216,768]{1,0:T(8,128)(2,1)} %copy-done.19, bf16[216,768]{1,0:T(8,128)(2,1)} %copy-done.17, ...), custom_call_target="tpu_custom_call" | custom-call | tf_op jit(solution)/shard_map/place/pallas_call | solution.py:191
  102.4 10.3 %attend.1 = (bf16[512,192]{1,0:T(8,128)(2,1)}, f32[3,4,1,128]{3,2,1,0:T(1,128)}) custom-call(bf16[512,192]{1,0:T(8,128)(2,1)} %slice.312.q_ref, bf16[1024,384]{1,0:T(8,128)(2,1)} %slice.313.kv_ref, f32[4,1,128]{2,1,0:T(1,128)} %bitcast.110, f32[1024,1]{1,0:T(8,128)} %copy.171.segk_ref), custom_call_target="tpu_custom_call" | custom-call | tf_op jit(solution)/shard_map/attend/pallas_call | solution.py:153
  117.9 5.1 %collective-permute-done.23 = bf16[128,768]{1,0:T(8,128)(2,1)S(1)} collective-permute-done((bf16[128,768]{1,0:T(8,128)(2,1)S(1)}, bf16[128,768]{1,0:T(8,128)(2,1)S(1)}, u32[]{:S(2)}, u32[]{:S(2)}) %collective-permute-start.23) | collective-permute-done | bytes 196640 | tf_op jit(solution)/shard_map/ppermute | solution.py:228
  124.8 5.8 %collective-permute-done.24 = bf16[128,768]{1,0:T(8,128)(2,1)} collective-permute-done((bf16[128,768]{1,0:T(8,128)(2,1)}, bf16[128,768]{1,0:T(8,128)(2,1)}, u32[]{:S(2)}, u32[]{:S(2)}) %collective-permute-start.24) | collective-permute-done | bytes 196640 | tf_op jit(solution)/shard_map/ppermute | solution.py:228
  132.3 5.0 %multiply_convert_fusion = (bf16[512,768]{1,0:T(8,128)(2,1)S(1)}, f32[512,768]{1,0:T(8,128)S(1)}, f32[512,768]{1,0:T(8,128)S(1)}) fusion(f32[768]{0:T(1024)S(1)} %add.194, bf16[768,768]{1,0:T(8,128)(2,1)S(1)} %bitcast.91, bf16[128,768]{1,0:T(8,128)(2,1)S(1)} %collective-permute-done.26, bf16[128,768]{1,0:T(8,128)(2,1)S(1)} %collective-permute-done.25, ...), kind=kOutput, calls=%fused_computation.6 | convolution fusion | flops 633077760 | bytes 5901312 | tf_op jit(solution)/shard_map/dot_general | solution.py:21
  141.3 4.3 %collective-permute-start.30 = (bf16[128,768]{1,0:T(8,128)(2,1)S(1)}, bf16[128,768]{1,0:T(8,128)(2,1)S(1)}, u32[]{:S(2)}, u32[]{:S(2)}) collective-permute-start(bf16[128,768]{1,0:T(8,128)(2,1)S(1)} %bitcast.115), channel_id=1, source_target_pairs={{0,0},{1,1},{2,8},{3,9},{4,16},{5,17},{6,24},{7,25},{8,2},{9,3},{1... | collective-permute-start | bytes 589832 | tf_op jit(solution)/shard_map/ppermute | solution.py:228
  148.4 7.4 %collective-permute-done.30 = bf16[128,768]{1,0:T(8,128)(2,1)S(1)} collective-permute-done((bf16[128,768]{1,0:T(8,128)(2,1)S(1)}, bf16[128,768]{1,0:T(8,128)(2,1)S(1)}, u32[]{:S(2)}, u32[]{:S(2)}) %collective-permute-start.30) | collective-permute-done | bytes 196640 | tf_op jit(solution)/shard_map/ppermute | solution.py:228
  156.4 5.6 %collective-permute-done.31 = bf16[128,768]{1,0:T(8,128)(2,1)S(1)} collective-permute-done((bf16[128,768]{1,0:T(8,128)(2,1)S(1)}, bf16[128,768]{1,0:T(8,128)(2,1)S(1)}, u32[]{:S(2)}, u32[]{:S(2)}) %collective-permute-start.31) | collective-permute-done | bytes 196640 | tf_op jit(solution)/shard_map/ppermute | solution.py:228
  168.7 6.7 %collective-permute-done.35 = bf16[128,768]{1,0:T(8,128)(2,1)S(1)} collective-permute-done((bf16[128,768]{1,0:T(8,128)(2,1)S(1)}, bf16[128,768]{1,0:T(8,128)(2,1)S(1)}, u32[]{:S(2)}, u32[]{:S(2)}) %collective-permute-start.35) | collective-permute-done | bytes 196640 | tf_op jit(solution)/shard_map/ppermute | solution.py:228
  180.4 3.6 %collective-permute-done.36 = bf16[128,768]{1,0:T(8,128)(2,1)S(1)} collective-permute-done((bf16[128,768]{1,0:T(8,128)(2,1)S(1)}, bf16[128,768]{1,0:T(8,128)(2,1)S(1)}, u32[]{:S(2)}, u32[]{:S(2)}) %collective-permute-start.36) | collective-permute-done | bytes 196640 | tf_op jit(solution)/shard_map/ppermute | solution.py:228
  184.0 3.1 convolution_convert_fusion.1
  187.1 3.6 %collective-permute-start.29 = (bf16[128,768]{1,0:T(8,128)(2,1)}, bf16[128,768]{1,0:T(8,128)(2,1)}, u32[]{:S(2)}, u32[]{:S(2)}) collective-permute-start(bf16[128,768]{1,0:T(8,128)(2,1)} %get-tuple-element.94), channel_id=1, source_target_pairs={{0,0},{1,1},{2,8},{3,9},{4,16},{5,17},{6,24},{7,25},{8,2},{9,3},{1... | collective-permute-start | bytes 589832 | tf_op jit(solution)/shard_map/ppermute | solution.py:228
  192.3 10.8 %attend_back.1 = (bf16[512,192]{1,0:T(8,128)(2,1)}, bf16[1024,384]{1,0:T(8,128)(2,1)}) custom-call(bf16[512,192]{1,0:T(8,128)(2,1)} %slice.312.q_ref, bf16[1024,384]{1,0:T(8,128)(2,1)} %slice.313.kv_ref, f32[4,1,128]{2,1,0:T(1,128)} %bitcast.111, f32[1024,1]{1,0:T(8,128)} %copy.171.segk_ref, f32[3,4,1,128]{3,2,1,0:T(1,128)} %get-tuple-element.36.lse_ref, ...), custom_call_target="tpu_custom_call" | custom-call | tf_op jit(solution)/shard_map/attend_back/pallas_call | solution.py:166
  203.2 3.6 %convolution_convert_fusion.2 = bf16[768,384]{1,0:T(8,128)(2,1)} fusion(bf16[1024,768]{1,0:T(8,128)(2,1)} %slice_dynamic-update-slice_fusion, bf16[1024,384]{1,0:T(8,128)(2,1)} %get-tuple-element.38), kind=kOutput, calls=%fused_computation.23 | convolution fusion | flops 604274688 | bytes 2949120 | tf_op jit(solution)/shard_map/dot_general | solution.py:21
  227.8 3.4 %unplace.3 = (bf16[216,768]{1,0:T(8,128)(2,1)}, bf16[216,768]{1,0:T(8,128)(2,1)}, bf16[216,768]{1,0:T(8,128)(2,1)}, bf16[216,768]{1,0:T(8,128)(2,1)}, bf16[216,7...) custom-call(s32[1]{0:T(128)} %bitcast.1.index_ref, ...), custom_call_target="tpu_custom_call" | custom-call | tf_op jit(solution)/shard_map/unplace/pallas_call | solution.py:209
  237.5 4.7 %collective-permute-done.51 = bf16[216,768]{1,0:T(8,128)(2,1)S(1)} collective-permute-done((bf16[216,768]{1,0:T(8,128)(2,1)}, bf16[216,768]{1,0:T(8,128)(2,1)S(1)}, u32[]{:S(2)}, u32[]{:S(2)}) %collective-permute-start.51) | collective-permute-done | bytes 331808 | tf_op jit(solution)/shard_map/ppermute | solution.py:228
  242.7 6.6 %collective-permute-done.53 = bf16[216,768]{1,0:T(8,128)(2,1)S(1)} collective-permute-done((bf16[216,768]{1,0:T(8,128)(2,1)}, bf16[216,768]{1,0:T(8,128)(2,1)S(1)}, u32[]{:S(2)}, u32[]{:S(2)}) %collective-permute-start.53) | collective-permute-done | bytes 331808 | tf_op jit(solution)/shard_map/ppermute | solution.py:228
  250.9 5.5 %collective-permute-done.55 = bf16[216,768]{1,0:T(8,128)(2,1)S(1)} collective-permute-done((bf16[216,768]{1,0:T(8,128)(2,1)}, bf16[216,768]{1,0:T(8,128)(2,1)S(1)}, u32[]{:S(2)}, u32[]{:S(2)}) %collective-permute-start.55) | collective-permute-done | bytes 331808 | tf_op jit(solution)/shard_map/ppermute | solution.py:228
  256.5 3.3 %collective-permute-start.56 = (bf16[216,768]{1,0:T(8,128)(2,1)S(1)}, bf16[216,768]{1,0:T(8,128)(2,1)S(1)}, u32[]{:S(2)}, u32[]{:S(2)}) collective-permute-start(bf16[216,768]{1,0:T(8,128)(2,1)S(1)} %add_convert_fusion.3), channel_id=1, source_target_pairs={{0,6},{1,7},{2,4},{3,5},{4,2},{5,3},{6,0},{7,1},{8,14},{9,15},{10,... | collective-permute-start | bytes 995336 | tf_op jit(solution)/shard_map/ppermute | solution.py:228
  259.8 10.9 %collective-permute-done.39 = bf16[512,384]{1,0:T(8,128)(2,1)S(1)} collective-permute-done((bf16[512,384]{1,0:T(8,128)(2,1)S(1)}, bf16[512,384]{1,0:T(8,128)(2,1)S(1)}, u32[]{:S(2)}, u32[]{:S(2)}) %collective-permute-start.39) | collective-permute-done | bytes 393248 | tf_op jit(solution)/shard_map/ppermute | solution.py:228
  275.5 3.4 %all-to-all-start.1 = ((bf16[4,24,1408]{2,1,0:T(8,128)(2,1)}), bf16[4,24,1408]{2,1,0:T(8,128)(2,1)S(1)}, u32[]{:S(2)}, u32[]{:S(2)}) async-start(bf16[4,24,1408]{2,1,0:T(8,128)(2,1)} %pad_maximum_fusion.6), calls=%async_computation.1 | async-start | bytes 540672 | tf_op jit(solution)/shard_map/all_to_all | solution.py:418
  280.1 3.3 %all-to-all-done.1 = bf16[4,24,1408]{2,1,0:T(8,128)(2,1)S(1)} async-done(((bf16[4,24,1408]{2,1,0:T(8,128)(2,1)}), bf16[4,24,1408]{2,1,0:T(8,128)(2,1)S(1)}, u32[]{:S(2)}, u32[]{:S(2)}) %all-to-all-start.1) | async-done | bytes 270368 | tf_op jit(solution)/shard_map/all_to_all | solution.py:418
  288.5 10.9 %collective-permute-start.42 = (bf16[128,768]{1,0:T(8,128)(2,1)S(1)}, bf16[128,768]{1,0:T(8,128)(2,1)S(1)}, u32[]{:S(2)}, u32[]{:S(2)}) collective-permute-start(bf16[128,768]{1,0:T(8,128)(2,1)S(1)} %fusion.30), channel_id=1, source_target_pairs={{0,0},{1,1},{2,8},{3,9},{4,16},{5,17},{6,24},{7,25},{8,2},{9,3},{1... | collective-permute-start | bytes 589832 | tf_op jit(solution)/shard_map/ppermute | solution.py:228
  301.0 5.3 %collective-permute-done.42 = bf16[128,768]{1,0:T(8,128)(2,1)S(1)} collective-permute-done((bf16[128,768]{1,0:T(8,128)(2,1)S(1)}, bf16[128,768]{1,0:T(8,128)(2,1)S(1)}, u32[]{:S(2)}, u32[]{:S(2)}) %collective-permute-start.42) | collective-permute-done | bytes 196640 | tf_op jit(solution)/shard_map/ppermute | solution.py:228
  (404 shorter events, 120.3 us)
Async XLA Ops:
  9.2 22.0 %collective-permute-start = (bf16[144,768]{1,0:T(8,128)(2,1)S(1)}, bf16[144,768]{1,0:T(8,128)(2,1)S(1)}, u32[]{:S(2)}, u32[]{:S(2)}) collective-permute-start(bf16[144,768]{1,0:T(8,128)(2,1)S(1)} %fusion.43), channel_id=1, source_target_pairs={{0,0},{1,1},{2,8},{3,9},{4,16},{5,17},{6,24},{7,25},{8,2},{9,3},{1... | collective-permute-start | bytes 663560 | tf_op jit(solution)/shard_map/ppermute | solution.py:228
  13.6 25.9 %collective-permute-start.9 = (bf16[4,24,640]{2,1,0:T(8,128)(2,1)S(1)}, bf16[4,24,640]{2,1,0:T(8,128)(2,1)S(1)}, u32[]{:S(2)}, u32[]{:S(2)}) collective-permute-start(bf16[4,24,640]{2,1,0:T(8,128)(2,1)S(1)} %slice.307.refs_0_), channel_id=1, source_target_pairs={{0,2},{1,3},{2,0},{3,1},{4,6},{5,7},{6,4},{7,5},{8,10},{9,11},{10,... | collective-permute-start | bytes 368648 | tf_op jit(solution)/shard_map/ppermute | solution.py:228
  15.3 25.1 %collective-permute-start.11 = (bf16[4,24,640]{2,1,0:T(8,128)(2,1)S(1)}, bf16[4,24,640]{2,1,0:T(8,128)(2,1)S(1)}, u32[]{:S(2)}, u32[]{:S(2)}) collective-permute-start(bf16[4,24,640]{2,1,0:T(8,128)(2,1)S(1)} %slice.307.refs_0_), channel_id=1, source_target_pairs={{0,4},{1,5},{2,6},{3,7},{4,0},{5,1},{6,2},{7,3},{8,12},{9,13},{10,... | collective-permute-start | bytes 368648 | tf_op jit(solution)/shard_map/ppermute | solution.py:228
  17.8 24.1 %collective-permute-start.13 = (bf16[4,24,640]{2,1,0:T(8,128)(2,1)S(1)}, bf16[4,24,640]{2,1,0:T(8,128)(2,1)S(1)}, u32[]{:S(2)}, u32[]{:S(2)}) collective-permute-start(bf16[4,24,640]{2,1,0:T(8,128)(2,1)S(1)} %slice.307.refs_0_), channel_id=1, source_target_pairs={{0,6},{1,7},{2,4},{3,5},{4,2},{5,3},{6,0},{7,1},{8,14},{9,15},{10,... | collective-permute-start | bytes 368648 | tf_op jit(solution)/shard_map/ppermute | solution.py:228
  39.5 20.6 %collective-permute-start.16 = (bf16[216,768]{1,0:T(8,128)(2,1)S(1)}, bf16[216,768]{1,0:T(8,128)(2,1)S(1)}, u32[]{:S(2)}, u32[]{:S(2)}) collective-permute-start(bf16[216,768]{1,0:T(8,128)(2,1)S(1)} %pad_maximum_fusion.5.refs_0_), channel_id=1, source_target_pairs={{0,2},{1,3},{2,0},{3,1},{4,6},{5,7},{6,4},{7,5},{8,10},{9,11},{10,... | collective-permute-start | bytes 995336 | tf_op jit(solution)/shard_map/ppermute | solution.py:228
  42.4 9.3 %collective-permute-start.14 = (bf16[4,24,640]{2,1,0:T(8,128)(2,1)S(1)}, bf16[4,24,640]{2,1,0:T(8,128)(2,1)S(1)}, u32[]{:S(2)}, u32[]{:S(2)}) collective-permute-start(bf16[4,24,640]{2,1,0:T(8,128)(2,1)S(1)} %collective-permute-done.13.refs_6_), channel_id=1, source_target_pairs={{0,1},{1,0},{2,3},{3,2},{4,5},{5,4},{6,7},{7,6},{8,9},{9,8},{10,11... | collective-permute-start | bytes 368648 | tf_op jit(solution)/shard_map/ppermute | solution.py:228
  44.7 25.8 %collective-permute-start.18 = (bf16[216,768]{1,0:T(8,128)(2,1)S(1)}, bf16[216,768]{1,0:T(8,128)(2,1)S(1)}, u32[]{:S(2)}, u32[]{:S(2)}) collective-permute-start(bf16[216,768]{1,0:T(8,128)(2,1)S(1)} %pad_maximum_fusion.5.refs_0_), channel_id=1, source_target_pairs={{0,4},{1,5},{2,6},{3,7},{4,0},{5,1},{6,2},{7,3},{8,12},{9,13},{10,... | collective-permute-start | bytes 995336 | tf_op jit(solution)/shard_map/ppermute | solution.py:228
  46.6 24.4 %collective-permute-start.20 = (bf16[216,768]{1,0:T(8,128)(2,1)S(1)}, bf16[216,768]{1,0:T(8,128)(2,1)S(1)}, u32[]{:S(2)}, u32[]{:S(2)}) collective-permute-start(bf16[216,768]{1,0:T(8,128)(2,1)S(1)} %pad_maximum_fusion.5.refs_0_), channel_id=1, source_target_pairs={{0,6},{1,7},{2,4},{3,5},{4,2},{5,3},{6,0},{7,1},{8,14},{9,15},{10,... | collective-permute-start | bytes 995336 | tf_op jit(solution)/shard_map/ppermute | solution.py:228
  49.2 27.4 %collective-permute-start.15 = (bf16[216,768]{1,0:T(8,128)(2,1)S(1)}, bf16[216,768]{1,0:T(8,128)(2,1)}, u32[]{:S(2)}, u32[]{:S(2)}) collective-permute-start(bf16[216,768]{1,0:T(8,128)(2,1)S(1)} %pad_maximum_fusion.5.refs_0_), channel_id=1, source_target_pairs={{0,1},{1,0},{2,3},{3,2},{4,5},{5,4},{6,7},{7,6},{8,9},{9,8},{10,11... | collective-permute-start | bytes 995336 | tf_op jit(solution)/shard_map/ppermute | solution.py:228
  56.6 16.0 %collective-permute-start.5 = (bf16[144,768]{1,0:T(8,128)(2,1)S(1)}, bf16[144,768]{1,0:T(8,128)(2,1)}, u32[]{:S(2)}, u32[]{:S(2)}) collective-permute-start(bf16[144,768]{1,0:T(8,128)(2,1)S(1)} %collective-permute-done.4), channel_id=1, source_target_pairs={{0,16},{1,17},{2,18},{3,19},{4,20},{5,21},{6,22},{7,23},{8,24},{9,... | collective-permute-start | bytes 663560 | tf_op jit(solution)/shard_map/ppermute | solution.py:228
  60.1 15.2 %collective-permute-start.6 = (bf16[144,768]{1,0:T(8,128)(2,1)S(1)}, bf16[144,768]{1,0:T(8,128)(2,1)S(1)}, u32[]{:S(2)}, u32[]{:S(2)}) collective-permute-start(bf16[144,768]{1,0:T(8,128)(2,1)S(1)} %collective-permute-done.4), channel_id=1, source_target_pairs={{0,8},{1,9},{2,10},{3,11},{4,12},{5,13},{6,14},{7,15},{8,0},{9,1},... | collective-permute-start | bytes 663560 | tf_op jit(solution)/shard_map/ppermute | solution.py:228
  70.5 10.7 %collective-permute-start.17 = (bf16[216,768]{1,0:T(8,128)(2,1)S(1)}, bf16[216,768]{1,0:T(8,128)(2,1)S(1)}, u32[]{:S(2)}, u32[]{:S(2)}) collective-permute-start(bf16[216,768]{1,0:T(8,128)(2,1)S(1)} %collective-permute-done.16.refs_2_), channel_id=1, source_target_pairs={{0,1},{1,0},{2,3},{3,2},{4,5},{5,4},{6,7},{7,6},{8,9},{9,8},{10,11... | collective-permute-start | bytes 995336 | tf_op jit(solution)/shard_map/ppermute | solution.py:228
  71.0 16.9 %collective-permute-start.19 = (bf16[216,768]{1,0:T(8,128)(2,1)S(1)}, bf16[216,768]{1,0:T(8,128)(2,1)S(1)}, u32[]{:S(2)}, u32[]{:S(2)}) collective-permute-start(bf16[216,768]{1,0:T(8,128)(2,1)S(1)} %collective-permute-done.18.refs_4_), channel_id=1, source_target_pairs={{0,1},{1,0},{2,3},{3,2},{4,5},{5,4},{6,7},{7,6},{8,9},{9,8},{10,11... | collective-permute-start | bytes 995336 | tf_op jit(solution)/shard_map/ppermute | solution.py:228
  72.5 19.0 %collective-permute-start.21 = (bf16[216,768]{1,0:T(8,128)(2,1)S(1)}, bf16[216,768]{1,0:T(8,128)(2,1)}, u32[]{:S(2)}, u32[]{:S(2)}) collective-permute-start(bf16[216,768]{1,0:T(8,128)(2,1)S(1)} %collective-permute-done.20.refs_6_), channel_id=1, source_target_pairs={{0,1},{1,0},{2,3},{3,2},{4,5},{5,4},{6,7},{7,6},{8,9},{9,8},{10,11... | collective-permute-start | bytes 995336 | tf_op jit(solution)/shard_map/ppermute | solution.py:228
  75.3 20.6 %collective-permute-start.7 = (bf16[144,768]{1,0:T(8,128)(2,1)}, bf16[144,768]{1,0:T(8,128)(2,1)S(1)}, u32[]{:S(2)}, u32[]{:S(2)}) collective-permute-start(bf16[144,768]{1,0:T(8,128)(2,1)} %collective-permute-done.5), channel_id=1, source_target_pairs={{0,8},{1,9},{2,10},{3,11},{4,12},{5,13},{6,14},{7,15},{8,0},{9,1},... | collective-permute-start | bytes 663560 | tf_op jit(solution)/shard_map/ppermute | solution.py:228
  141.3 14.5 %collective-permute-start.30 = (bf16[128,768]{1,0:T(8,128)(2,1)S(1)}, bf16[128,768]{1,0:T(8,128)(2,1)S(1)}, u32[]{:S(2)}, u32[]{:S(2)}) collective-permute-start(bf16[128,768]{1,0:T(8,128)(2,1)S(1)} %bitcast.115), channel_id=1, source_target_pairs={{0,0},{1,1},{2,8},{3,9},{4,16},{5,17},{6,24},{7,25},{8,2},{9,3},{1... | collective-permute-start | bytes 589832 | tf_op jit(solution)/shard_map/ppermute | solution.py:228
  180.3 10.4 %collective-permute-start.37 = (bf16[128,768]{1,0:T(8,128)(2,1)S(1)}, bf16[128,768]{1,0:T(8,128)(2,1)S(1)}, u32[]{:S(2)}, u32[]{:S(2)}) collective-permute-start(bf16[128,768]{1,0:T(8,128)(2,1)S(1)} %get-tuple-element.81), channel_id=1, source_target_pairs={{0,8},{1,9},{2,10},{3,11},{4,12},{5,13},{6,14},{7,15},{8,0},{9,1},... | collective-permute-start | bytes 589832 | tf_op jit(solution)/shard_map/ppermute | solution.py:228
  187.1 44.2 %collective-permute-start.29 = (bf16[128,768]{1,0:T(8,128)(2,1)}, bf16[128,768]{1,0:T(8,128)(2,1)}, u32[]{:S(2)}, u32[]{:S(2)}) collective-permute-start(bf16[128,768]{1,0:T(8,128)(2,1)} %get-tuple-element.94), channel_id=1, source_target_pairs={{0,0},{1,1},{2,8},{3,9},{4,16},{5,17},{6,24},{7,25},{8,2},{9,3},{1... | collective-permute-start | bytes 589832 | tf_op jit(solution)/shard_map/ppermute | solution.py:228
  215.2 9.6 %collective-permute-start.48 = (bf16[4,24,640]{2,1,0:T(8,128)(2,1)}, bf16[4,24,640]{2,1,0:T(8,128)(2,1)S(1)}, u32[]{:S(2)}, u32[]{:S(2)}) collective-permute-start(bf16[4,24,640]{2,1,0:T(8,128)(2,1)} %get-tuple-element.46), channel_id=1, source_target_pairs={{0,1},{1,0},{2,3},{3,2},{4,5},{5,4},{6,7},{7,6},{8,9},{9,8},{10,11... | collective-permute-start | bytes 368648 | tf_op jit(solution)/shard_map/ppermute | solution.py:228
  216.3 16.1 %collective-permute-start.43 = (bf16[4,24,640]{2,1,0:T(8,128)(2,1)}, bf16[4,24,640]{2,1,0:T(8,128)(2,1)}, u32[]{:S(2)}, u32[]{:S(2)}) collective-permute-start(bf16[4,24,640]{2,1,0:T(8,128)(2,1)} %get-tuple-element.40), channel_id=1, source_target_pairs={{0,1},{1,0},{2,3},{3,2},{4,5},{5,4},{6,7},{7,6},{8,9},{9,8},{10,11... | collective-permute-start | bytes 368648 | tf_op jit(solution)/shard_map/ppermute | solution.py:228
  219.6 13.9 %collective-permute-start.45 = (bf16[4,24,640]{2,1,0:T(8,128)(2,1)S(1)}, bf16[4,24,640]{2,1,0:T(8,128)(2,1)S(1)}, u32[]{:S(2)}, u32[]{:S(2)}) collective-permute-start(bf16[4,24,640]{2,1,0:T(8,128)(2,1)S(1)} %add_convert_fusion.10), channel_id=1, source_target_pairs={{0,2},{1,3},{2,0},{3,1},{4,6},{5,7},{6,4},{7,5},{8,10},{9,11},{10,... | collective-permute-start | bytes 368648 | tf_op jit(solution)/shard_map/ppermute | solution.py:228
  222.2 12.3 %collective-permute-start.47 = (bf16[4,24,640]{2,1,0:T(8,128)(2,1)S(1)}, bf16[4,24,640]{2,1,0:T(8,128)(2,1)S(1)}, u32[]{:S(2)}, u32[]{:S(2)}) collective-permute-start(bf16[4,24,640]{2,1,0:T(8,128)(2,1)S(1)} %add_convert_fusion.9), channel_id=1, source_target_pairs={{0,4},{1,5},{2,6},{3,7},{4,0},{5,1},{6,2},{7,3},{8,12},{9,13},{10,... | collective-permute-start | bytes 368648 | tf_op jit(solution)/shard_map/ppermute | solution.py:228
  225.5 10.0 %collective-permute-start.49 = (bf16[4,24,640]{2,1,0:T(8,128)(2,1)}, bf16[4,24,640]{2,1,0:T(8,128)(2,1)S(1)}, u32[]{:S(2)}, u32[]{:S(2)}) collective-permute-start(bf16[4,24,640]{2,1,0:T(8,128)(2,1)} %add_convert_fusion.8), channel_id=1, source_target_pairs={{0,6},{1,7},{2,4},{3,5},{4,2},{5,3},{6,0},{7,1},{8,14},{9,15},{10,... | collective-permute-start | bytes 368648 | tf_op jit(solution)/shard_map/ppermute | solution.py:228
  231.2 10.9 %collective-permute-start.51 = (bf16[216,768]{1,0:T(8,128)(2,1)}, bf16[216,768]{1,0:T(8,128)(2,1)S(1)}, u32[]{:S(2)}, u32[]{:S(2)}) collective-permute-start(bf16[216,768]{1,0:T(8,128)(2,1)} %get-tuple-element.50), channel_id=1, source_target_pairs={{0,1},{1,0},{2,3},{3,2},{4,5},{5,4},{6,7},{7,6},{8,9},{9,8},{10,11... | collective-permute-start | bytes 995336 | tf_op jit(solution)/shard_map/ppermute | solution.py:228
  232.4 16.9 %collective-permute-start.53 = (bf16[216,768]{1,0:T(8,128)(2,1)}, bf16[216,768]{1,0:T(8,128)(2,1)S(1)}, u32[]{:S(2)}, u32[]{:S(2)}) collective-permute-start(bf16[216,768]{1,0:T(8,128)(2,1)} %get-tuple-element.52), channel_id=1, source_target_pairs={{0,1},{1,0},{2,3},{3,2},{4,5},{5,4},{6,7},{7,6},{8,9},{9,8},{10,11... | collective-permute-start | bytes 995336 | tf_op jit(solution)/shard_map/ppermute | solution.py:228
  233.5 22.9 %collective-permute-start.55 = (bf16[216,768]{1,0:T(8,128)(2,1)}, bf16[216,768]{1,0:T(8,128)(2,1)S(1)}, u32[]{:S(2)}, u32[]{:S(2)}) collective-permute-start(bf16[216,768]{1,0:T(8,128)(2,1)} %get-tuple-element.54), channel_id=1, source_target_pairs={{0,1},{1,0},{2,3},{3,2},{4,5},{5,4},{6,7},{7,6},{8,9},{9,8},{10,11... | collective-permute-start | bytes 995336 | tf_op jit(solution)/shard_map/ppermute | solution.py:228
  234.5 37.2 %collective-permute-start.50 = (bf16[216,768]{1,0:T(8,128)(2,1)}, bf16[216,768]{1,0:T(8,128)(2,1)S(1)}, u32[]{:S(2)}, u32[]{:S(2)}) collective-permute-start(bf16[216,768]{1,0:T(8,128)(2,1)} %get-tuple-element.48), channel_id=1, source_target_pairs={{0,1},{1,0},{2,3},{3,2},{4,5},{5,4},{6,7},{7,6},{8,9},{9,8},{10,11... | collective-permute-start | bytes 995336 | tf_op jit(solution)/shard_map/ppermute | solution.py:228
  235.5 35.1 %collective-permute-start.39 = (bf16[512,384]{1,0:T(8,128)(2,1)S(1)}, bf16[512,384]{1,0:T(8,128)(2,1)S(1)}, u32[]{:S(2)}, u32[]{:S(2)}) collective-permute-start(bf16[512,384]{1,0:T(8,128)(2,1)S(1)} %slice.277), channel_id=1, source_target_pairs={{0,1},{1,0},{2,3},{3,2},{4,5},{5,4},{6,7},{7,6},{8,9},{9,8},{10,11... | collective-permute-start | bytes 1179656 | tf_op jit(solution)/shard_map/ppermute | solution.py:228
  242.3 29.5 %collective-permute-start.52 = (bf16[216,768]{1,0:T(8,128)(2,1)S(1)}, bf16[216,768]{1,0:T(8,128)(2,1)S(1)}, u32[]{:S(2)}, u32[]{:S(2)}) collective-permute-start(bf16[216,768]{1,0:T(8,128)(2,1)S(1)} %add_convert_fusion.5), channel_id=1, source_target_pairs={{0,2},{1,3},{2,0},{3,1},{4,6},{5,7},{6,4},{7,5},{8,10},{9,11},{10,... | collective-permute-start | bytes 995336 | tf_op jit(solution)/shard_map/ppermute | solution.py:228
  249.4 23.7 %collective-permute-start.54 = (bf16[216,768]{1,0:T(8,128)(2,1)S(1)}, bf16[216,768]{1,0:T(8,128)(2,1)S(1)}, u32[]{:S(2)}, u32[]{:S(2)}) collective-permute-start(bf16[216,768]{1,0:T(8,128)(2,1)S(1)} %add_convert_fusion.4), channel_id=1, source_target_pairs={{0,4},{1,5},{2,6},{3,7},{4,0},{5,1},{6,2},{7,3},{8,12},{9,13},{10,... | collective-permute-start | bytes 995336 | tf_op jit(solution)/shard_map/ppermute | solution.py:228
  256.5 16.6 %collective-permute-start.56 = (bf16[216,768]{1,0:T(8,128)(2,1)S(1)}, bf16[216,768]{1,0:T(8,128)(2,1)S(1)}, u32[]{:S(2)}, u32[]{:S(2)}) collective-permute-start(bf16[216,768]{1,0:T(8,128)(2,1)S(1)} %add_convert_fusion.3), channel_id=1, source_target_pairs={{0,6},{1,7},{2,4},{3,5},{4,2},{5,3},{6,0},{7,1},{8,14},{9,15},{10,... | collective-permute-start | bytes 995336 | tf_op jit(solution)/shard_map/ppermute | solution.py:228
  288.5 17.9 %collective-permute-start.42 = (bf16[128,768]{1,0:T(8,128)(2,1)S(1)}, bf16[128,768]{1,0:T(8,128)(2,1)S(1)}, u32[]{:S(2)}, u32[]{:S(2)}) collective-permute-start(bf16[128,768]{1,0:T(8,128)(2,1)S(1)} %fusion.30), channel_id=1, source_target_pairs={{0,0},{1,1},{2,8},{3,9},{4,16},{5,17},{6,24},{7,25},{8,2},{9,3},{1... | collective-permute-start | bytes 589832 | tf_op jit(solution)/shard_map/ppermute | solution.py:228
  (102 other events, 772.2 us)
